TPU v7x, 128 devices: a whole 4x4x4 slice. The times are simulated.
128 devices in a mesh: section: 4 (over z), space: 32 (over x, y, core).
Axes of the slice: x: 4, y: 4, z: 4, core: 2. Of those that a mesh axis runs over, the one named last changes fastest.
Arguments:
- features: bfloat16 [4, 128, 784, 256], P('section', 'space')
- tissue: int32 [4, 128], P('section'), may hold values from 0 to 1, as said below
- first_weight: bfloat16 [256, 512], replicated, may hold values from -0.375 to 0.375
- first_gain: float32 [512], replicated, may hold values from 0.1 to 1.9
- first_bias: float32 [512], replicated, may hold values from -3 to 3
- second_weight: bfloat16 [512, 1024], P(None, 'space'), may hold values from -0.25 to 0.25
- second_gain: float32 [1024], replicated, may hold values from 0.1 to 1.9
- second_bias: float32 [1024], replicated, may hold values from -3 to 3
Outputs:
- output: bfloat16 [4, 1024, 100352], P('section', 'space')
- first_mean: float32 [512], replicated
- first_var: float32 [512], replicated
- second_mean: float32 [1024], P('space')
- second_var: float32 [1024], P('space')
Inputs may be any that keep to these rules, and one draw needn't show every extreme that they name: Every tile row holds at least one tissue tile and at least one tile without tissue.
All inputs are finite; a program needn't handle non-finite values.
Results may differ from a plain program's by a relative error of at most 0.0053.
Values may be sent and summed in bfloat16 or wider, within the bound.
No kernel may reach another device: no remote copies, remote signals or barrier semaphores. Data moves between devices by JAX's collectives and lax.ppermute only.
A program may use at most 128 MiB of HBM per device.

v0:
```python
import jax
import jax.numpy as jnp
from jax import lax
from jax.sharding import PartitionSpec as P

EPS = 1e-05


def normalize(values, mean_val, var_val, gain, bias):
    return jnp.maximum(gain * (values - mean_val) * lax.rsqrt(var_val + EPS) + bias, 0.0)


def masked_sum(values, weight):
    return jnp.sum(values * weight, axis=(0, 1, 2))


def masked_squares(values, weight, mean_val):
    centred = values - mean_val
    return jnp.sum(weight * centred * centred, axis=(0, 1, 2))


def channel_first(values):
    batch, tiles_here, pixels, chans = values.shape
    return jnp.transpose(values, (0, 3, 1, 2)).reshape(batch, chans, tiles_here * pixels)


def shards(
    features, tissue, first_weight, first_gain, first_bias, second_weight, second_gain, second_bias
):
    index = lax.axis_index("space")
    tiles_here = features.shape[1]
    pixels = features.shape[2]
    row_mask = tissue[0].astype(jnp.float32)
    own_mask = lax.dynamic_slice_in_dim(row_mask, index * tiles_here, tiles_here)
    own_weight = own_mask[None, :, None, None]
    local_count = jnp.sum(own_mask) * pixels
    first = jnp.einsum("mtpc,cd->mtpd", features, first_weight, preferred_element_type=jnp.float32)
    total, count = lax.psum((masked_sum(first, own_weight), local_count), ("section", "space"))
    first_mean = total / count
    first_var = (
        lax.psum(masked_squares(first, own_weight, first_mean), ("section", "space")) / count
    )
    activation = normalize(first, first_mean, first_var, first_gain, first_bias).astype(
        jnp.bfloat16
    )
    second = jnp.einsum(
        "mtpc,cd->mtpd",
        activation,
        lax.all_gather(second_weight, "space", axis=1, tiled=True),
        preferred_element_type=jnp.float32,
    )
    width_here = second_weight.shape[1]
    moved = lax.all_to_all(channel_first(second), "space", split_axis=1, concat_axis=2, tiled=True)
    row_weight = jnp.repeat(row_mask, pixels)[None, None, :]
    second_mean = lax.psum(jnp.sum(moved * row_weight, axis=(0, 2)), "section") / count
    centred = moved - second_mean[:, None]
    second_var = lax.psum(jnp.sum(row_weight * centred * centred, axis=(0, 2)), "section") / count
    gain_here = lax.dynamic_slice_in_dim(second_gain, index * width_here, width_here)
    bias_here = lax.dynamic_slice_in_dim(second_bias, index * width_here, width_here)
    output = normalize(
        moved, second_mean[:, None], second_var[:, None], gain_here[:, None], bias_here[:, None]
    ).astype(jnp.bfloat16)
    return (output, first_mean, first_var, second_mean, second_var)


def solution(mesh):
    in_specs = (
        P("section", "space", None, None),
        P("section", None),
        P(),
        P(),
        P(),
        P(None, "space"),
        P(),
        P(),
    )
    out_specs = (P("section", "space", None), P(), P(), P("space"), P("space"))
    return jax.shard_map(shards, mesh=mesh, in_specs=in_specs, out_specs=out_specs, check_vma=False)
```

profile of v0, /device:TPU:44, one launch (start us, length us, event | category | flops | bytes accessed | tf_op | source)
XLA Modules:
  0.0 490.6 jit_solution(13047732161503273822)
XLA Ops:
  7.2 0.7 all-gather.2.cloned.1.call-update
  8.6 0.7 fusion.12
  9.9 4.7 multiply_reduce_fusion.1
  14.6 64.0 %all-reduce = (f32[512]{0:T(512)S(1)}, f32[]{:T(128)}) all-reduce(f32[512]{0:T(512)S(1)} %get-tuple-element.13, f32[]{:T(128)S(6)} %mul.112), channel_id=1, replica_groups=mesh['section'=4,'space'=32] {'section','space'}, use_global_device_ids=true, to_apply=%region_1.0 | all-reduce | flops 513 | bytes 4104 | tf_op jit(solution)/shard_map/psum | solution.py:38
  78.6 0.7 broadcast_divide_fusion.1
  79.3 3.9 fusion.1
  83.2 62.5 %psum.37 = f32[512]{0:T(512)S(1)} all-reduce(f32[512]{0:T(512)S(1)} %fusion.1), channel_id=1, replica_groups=mesh['section'=4,'space'=32] {'section','space'}, use_global_device_ids=true, to_apply=%region_5.0 | all-reduce | flops 512 | bytes 4096 | tf_op jit(solution)/shard_map/psum | solution.py:41
  145.7 1.3 add_rsqrt_fusion
  147.0 11.2 %fusion.2 = f32[4,784,1024]{2,1,0:T(8,128)} fusion(f32[4,784,512]{2,1,0:T(8,128)} %get-tuple-element.14, f32[512]{0:T(512)S(1)} %copy-done.4, f32[512]{0:T(512)S(1)} %get-tuple-element.9, f32[512]{0:T(512)S(1)} %broadcast_divide_fusion.1, f32[512]{0:T(512)S(1)} %copy-done.5, bf16[512,1024]{0,1:T(8,128)(2,1)} %all-gather.2.cloned.1.call-done), kind=kOutput, calls=%fused_computation.8 | convolution fusion | flops 3297968128 | bytes 20324352 | tf_op jit(solution)/shard_map/mtpc,cd->mtpd/dot_general | solution.py:46
  158.2 27.1 %copy.17 = f32[1,1024,3136]{2,0,1:T(1,128)} copy(f32[1,1024,3136]{1,2,0:T(8,128)} %bitcast.28) | data formatting | bytes 25690112 | tf_op jit(solution)/shard_map/reshape | solution.py:24
  185.3 8.8 %all-to-all-start = ((f32[1,1024,3136]{2,0,1:T(1,128)}), f32[1,1024,3136]{2,0,1:T(1,128)}, u32[]{:S(2)}, u32[]{:S(2)}) async-start(f32[1,1024,3136]{2,0,1:T(1,128)} %copy.17), calls=%async_computation | async-start | bytes 26214400 | tf_op jit(solution)/shard_map/all_to_all | solution.py:53
  194.6 0.8 dynamic_slice.11
  195.4 0.8 dynamic_slice.14
  196.2 204.3 %all-to-all-done = f32[1,1024,3136]{2,0,1:T(1,128)} async-done(((f32[1,1024,3136]{2,0,1:T(1,128)}), f32[1,1024,3136]{2,0,1:T(1,128)}, u32[]{:S(2)}, u32[]{:S(2)}) %all-to-all-start) | async-done | bytes 12845088 | tf_op jit(solution)/shard_map/all_to_all | solution.py:53
  400.4 10.3 %copy.19 = f32[1,1024,3136]{2,1,0:T(8,128)} copy(f32[1,1024,3136]{2,0,1:T(1,128)} %all-to-all-done) | data formatting | bytes 25690112
  410.7 17.0 %copy.18 = f32[1,32,32,3136]{3,2,1,0:T(8,128)} copy(f32[1,32,32,3136]{3,1,2,0:T(8,128)} %bitcast.25) | data formatting | bytes 25690112 | tf_op jit(solution)/shard_map/all_to_all | solution.py:53
  427.7 5.7 %multiply_reduce_fusion = f32[32]{0:T(128)S(1)} fusion(f32[1,32,32,3136]{3,1,2,0:T(8,128)} %bitcast.26, f32[32,3136]{1,0:T(8,128)S(1)} %broadcast_in_dim.5), kind=kLoop, calls=%fused_computation.2 | loop fusion | flops 6422496 | bytes 13246592 | tf_op jit(solution)/shard_map/reduce_sum | solution.py:55
  433.4 9.0 %psum.38 = f32[32]{0:T(128)S(1)} all-reduce(f32[32]{0:T(128)S(1)} %multiply_reduce_fusion), channel_id=1, replica_groups=mesh['section'=4,'space'=32] {'section'}, use_global_device_ids=true, to_apply=%region_7.0 | all-reduce | flops 32 | bytes 256 | tf_op jit(solution)/shard_map/psum | solution.py:55
  442.4 0.7 broadcast_divide_fusion.3
  443.1 6.6 %fusion = f32[32]{0:T(128)S(1)} fusion(f32[1,32,32,3136]{3,1,2,0:T(8,128)} %bitcast.27, f32[32]{0:T(128)S(1)} %broadcast_divide_fusion.3, f32[32,3136]{1,0:T(8,128)S(1)} %broadcast_in_dim.5), kind=kLoop, calls=%fused_computation.1 | loop fusion | flops 12845024 | bytes 13246720 | tf_op jit(solution)/shard_map/reduce_sum | solution.py:57
  449.7 9.9 %psum.39 = f32[32]{0:T(128)S(1)} all-reduce(f32[32]{0:T(128)S(1)} %fusion), channel_id=1, replica_groups=mesh['section'=4,'space'=32] {'section'}, use_global_device_ids=true, to_apply=%region_9.0 | all-reduce | flops 32 | bytes 256 | tf_op jit(solution)/shard_map/psum | solution.py:57
  459.6 1.2 add_rsqrt_fusion.1
  460.8 12.9 %all_to_all.16 = f32[1,32,100352]{2,1,0:T(8,128)} reshape(f32[1,32,32,3136]{3,2,1,0:T(8,128)} %copy.18) | data formatting | bytes 25690112 | tf_op jit(solution)/shard_map/all_to_all | solution.py:53
  473.7 10.0 %maximum_convert_fusion = bf16[1,32,100352]{2,1,0:T(8,128)(2,1)} fusion(f32[1,32,100352]{2,1,0:T(8,128)} %all_to_all.16, f32[32]{0:T(128)S(1)} %dynamic_slice.14, f32[32]{0:T(128)S(1)} %get-tuple-element.7, f32[32]{0:T(128)S(1)} %broadcast_divide_fusion.3, f32[32]{0:T(128)S(1)} %dynamic_slice.11), kind=kLoop, calls=%fused_computation.3 | loop fusion | flops 19267584 | bytes 19268096 | tf_op jit(solution)/shard_map/convert_element_type | solution.py:62
  (21 shorter events, 1.2 us)
Async XLA Ops:
  7.2 2.7 copy-start
  7.2 139.8 %all-gather.2.cloned.1.call-start = ((), (), s32[]{:S(2)}) async-start(), calls=%async_computation.1 | async-start | bytes 1081344 | tf_op jit(solution)/shard_map/all_gather | solution.py:49
  14.6 132.3 %copy-start.4 = (f32[512]{0:T(512)S(1)}, f32[512]{0:T(512)}, u32[]{:S(2)}) copy-start(f32[512]{0:T(512)} %param.12) | copy-start | bytes 6148
  14.6 132.4 %copy-start.5 = (f32[512]{0:T(512)S(1)}, f32[512]{0:T(512)}, u32[]{:S(2)}) copy-start(f32[512]{0:T(512)} %param.11) | copy-start | bytes 6148
  79.3 78.9 %copy-start.2 = (f32[512]{0:T(512)}, f32[512]{0:T(512)S(1)}, u32[]{:S(2)}) copy-start(f32[512]{0:T(512)S(1)} %broadcast_divide_fusion.1) | copy-start | bytes 6148
  185.3 8.8 %copy-start.6 = (s32[1,128]{1,0:T(1,128)S(1)}, s32[1,128]{1,0:T(1,128)}, u32[]{:S(2)}) copy-start(s32[1,128]{1,0:T(1,128)} %param.9) | copy-start | bytes 1540
  185.3 215.1 %all-to-all-start = ((f32[1,1024,3136]{2,0,1:T(1,128)}), f32[1,1024,3136]{2,0,1:T(1,128)}, u32[]{:S(2)}, u32[]{:S(2)}) async-start(f32[1,1024,3136]{2,0,1:T(1,128)} %copy.17), calls=%async_computation | async-start | bytes 26214400 | tf_op jit(solution)/shard_map/all_to_all | solution.py:53
  443.1 30.7 %copy-start.3 = (f32[32]{0:T(128)}, f32[32]{0:T(128)S(1)}, u32[]{:S(2)}) copy-start(f32[32]{0:T(128)S(1)} %broadcast_divide_fusion.3) | copy-start | bytes 388
  473.7 10.0 %copy-start.1 = (bf16[1,4,784,256]{3,2,1,0:T(8,128)(2,1)S(1)}, bf16[1,4,784,256]{3,2,1,0:T(8,128)(2,1)}, u32[]{:S(2)}) copy-start(bf16[1,4,784,256]{3,2,1,0:T(8,128)(2,1)} %param.8) | copy-start | bytes 4816900
Sparse Core Ops, SparseCore 0:
  10.3 42.4 all-gather.1
where the time goes:
time: 492 us; the launch traced here: 491 us
  waiting for transfers between devices  205 us (42%)
  blocking collectives  145 us (29%)
  local copies, waits for them, and re-layouts  69.3 us (14%)
  other arithmetic  31.4 us (6%)
  matrix products  15.9 us (3%)
  between operations  14.8 us (3%)
  starting transfers between devices  8.84 us (2%)
    all_to_all x1, waiting for transfers between devices, shards(): lax.all_to_all(channel_first(second), 'space', split_axis=1, concat_axis=...  204 us
    psum x1, blocking collectives, shards(): lax.psum((masked_sum(first, own_weight), local_count), ('section', 'space'))  64 us
    psum x1, blocking collectives, shards(): lax.psum(masked_squares(first, own_weight, first_mean), ('section', 'spac...  62.5 us
    all_to_all x2, local copies, waits for them, and re-layouts, shards(): lax.all_to_all(channel_first(second), 'space', split_axis=1, concat_axis=...  29.9 us
    reshape x1, local copies, waits for them, and re-layouts, channel_first(): jnp.transpose(values, (0, 3, 1, 2))  27.1 us
    dot_general x1, matrix products, shards(): jnp.einsum('mtpc,cd->mtpd', activation, lax.all_gather(second_weight, 'sp...  11.2 us
    unnamed x15, local copies, waits for them, and re-layouts  10.3 us
    convert_element_type x1, other arithmetic, shards(): output = normalize(moved, second_mean[:, None], second_var[:, None], gain...  9.96 us
  transfers between devices with their start and end apart: 2, of which 1 were waited for; matrix products, arithmetic and copies ran while one was open for 3% of the time, Pallas kernels for 0%

commit v1 on v0

v1 whole, which is shorter than its diff:
```python
import jax
import jax.numpy as jnp
from jax import lax
from jax.sharding import Mesh
from jax.sharding import PartitionSpec as P

EPS = 1e-05
EVERY = ("z", "x", "y", "c")
PLANE = ("x", "y", "c")


def all_sum(values, axes):
    for axis in axes:
        values = lax.psum(values, (axis,))
    return values


def shards(
    features, tissue, first_weight, first_gain, first_bias, second_weight, second_gain, second_bias
):
    index = lax.axis_index(PLANE)
    tiles_here, pixels, depth = features.shape[1:]
    rows = features.reshape(tiles_here * pixels, depth)
    row_mask = tissue[0].astype(jnp.float32)
    own_mask = lax.dynamic_slice_in_dim(row_mask, index * tiles_here, tiles_here)
    own_weight = jnp.repeat(own_mask, pixels)
    first = jnp.dot(rows, first_weight, preferred_element_type=jnp.float32)
    total, count = all_sum(
        (jnp.sum(first * own_weight[:, None], axis=0), jnp.sum(own_mask) * pixels), EVERY
    )
    first_mean = total / count
    centred = first - first_mean
    first_var = all_sum(jnp.sum(own_weight[:, None] * centred * centred, axis=0), EVERY) / count
    activation = jnp.maximum(
        first_gain * centred * lax.rsqrt(first_var + EPS) + first_bias, 0.0
    ).astype(jnp.bfloat16)
    weights = lax.all_gather(second_weight, PLANE, axis=1, tiled=True)
    second = lax.dot_general(
        weights, activation, (((0,), (1,)), ((), ())), preferred_element_type=jnp.float32
    )
    centre = jnp.mean(second, axis=1)
    shifted = second - centre[:, None]
    tissue_sum = jnp.sum(shifted * own_weight, axis=1)
    tissue_squares = jnp.sum(shifted * shifted * own_weight, axis=1)
    width = second_weight.shape[1]
    moved = lax.all_to_all(
        shifted.astype(jnp.bfloat16).reshape(-1, width, tiles_here * pixels),
        PLANE,
        split_axis=0,
        concat_axis=0,
        tiled=True,
    )
    parts = lax.all_to_all(
        jnp.stack([centre, tissue_sum, tissue_squares], axis=1).reshape(-1, width, 3),
        PLANE,
        split_axis=0,
        concat_axis=0,
        tiled=True,
    )
    centres, sums, squares = parts[..., 0], parts[..., 1], parts[..., 2]
    held = (jnp.sum(row_mask.reshape(-1, tiles_here), axis=1) * pixels)[:, None]
    second_mean = all_sum(jnp.sum(sums + held * centres, axis=0), ("z",)) / count
    offset = centres - second_mean
    second_var = (
        all_sum(
            jnp.sum(squares + 2.0 * offset * sums + held * offset * offset, axis=0), ("z",)
        )
        / count
    )
    gain_here = lax.dynamic_slice_in_dim(second_gain, index * width, width)
    bias_here = lax.dynamic_slice_in_dim(second_bias, index * width, width)
    scale = gain_here * lax.rsqrt(second_var + EPS)
    output = jnp.maximum(
        (moved.astype(jnp.float32) + offset[..., None]) * scale[:, None] + bias_here[:, None], 0.0
    ).astype(jnp.bfloat16)
    output = jnp.transpose(output, (1, 0, 2)).reshape(1, width, -1)
    return (output, first_mean, first_var, second_mean, second_var)


def solution(mesh):
    fine = Mesh(mesh.devices.reshape(4, 4, 4, 2), EVERY)
    in_specs = (
        P("z", PLANE, None, None),
        P("z", None),
        P(),
        P(),
        P(),
        P(None, PLANE),
        P(),
        P(),
    )
    out_specs = (P("z", PLANE, None), P(), P(), P(PLANE), P(PLANE))
    return jax.shard_map(shards, mesh=fine, in_specs=in_specs, out_specs=out_specs, check_vma=False)
```

time: 492 us -> 250 us (0.51)
  waiting for transfers between devices: 205 us -> 68.5 us
  blocking collectives: 145 us -> 79.9 us
  local copies, waits for them, and re-layouts: 69.3 us -> 26 us
  other arithmetic: 31.4 us -> 25.9 us
  starting transfers between devices: 8.84 us -> 14.3 us
    all_to_all x1 -> x2, waiting for transfers between devices: 204 us -> 67.8 us  [the longest x1 67.8 us: shards(): lax.all_to_all(shifted.astype(jnp.bfloat16).reshape(-1, width, tiles_here...]
    psum x4 -> x10, blocking collectives: 145 us -> 79.9 us  [all_sum(): values = lax.psum(values, (axis,))]
    all_to_all x2 -> x0, local copies, waits for them, and re-layouts: 29.9 us -> none  [shards(): lax.all_to_all(channel_first(second), 'space', split_axis=1, concat_axis=...]
    reshape x1, local copies, waits for them, and re-layouts: 27.1 us -> 10.8 us  [shards(): output = jnp.transpose(output, (1, 0, 2)).reshape(1, width, -1)]
    unnamed x15 -> x12, local copies, waits for them, and re-layouts: 10.3 us -> 0.03 us
    convert_element_type x1 -> x0, other arithmetic: 9.96 us -> none  [shards(): output = normalize(moved, second_mean[:, None], second_var[:, None], gain...]
    convert_element_type x0 -> x1, local copies, waits for them, and re-layouts: none -> 9.21 us  [shards(): shifted.astype(jnp.bfloat16).reshape(-1, width, tiles_here * pixels)]
    transpose x0 -> x1, other arithmetic: none -> 6.24 us  [shards(): output = jnp.transpose(output, (1, 0, 2)).reshape(1, width, -1)]
  transfers between devices with their start and end apart: 2 -> 3, of which waited for: 1 -> 1; matrix products, arithmetic and copies ran while one was open for 3% -> 10% of each run, Pallas kernels for 0% -> 0%
where the time goes in v1:
time: 250 us; the launch traced here: 245 us
  blocking collectives  79.9 us (32%)
  waiting for transfers between devices  68.5 us (27%)
  local copies, waits for them, and re-layouts  26 us (10%)
  other arithmetic  25.9 us (10%)
  matrix products  15.8 us (6%)
  between operations  14.8 us (6%)
  starting transfers between devices  14.3 us (6%)
    psum x10, blocking collectives, all_sum(): values = lax.psum(values, (axis,))  79.9 us
    all_to_all x1, waiting for transfers between devices, shards(): lax.all_to_all(shifted.astype(jnp.bfloat16).reshape(-1, width, tiles_here...  67.8 us
    dot_general x1, matrix products, shards(): lax.dot_general(weights, activation, (((0,), (1,)), ((), ())), preferred_...  11.4 us
    reshape x1, local copies, waits for them, and re-layouts, shards(): output = jnp.transpose(output, (1, 0, 2)).reshape(1, width, -1)  10.8 us
    reduce_sum x1, other arithmetic, shards(): tissue_sum = jnp.sum(shifted * own_weight, axis=1)  9.5 us
    convert_element_type x1, local copies, waits for them, and re-layouts, shards(): shifted.astype(jnp.bfloat16).reshape(-1, width, tiles_here * pixels)  9.21 us
    all_to_all x1, starting transfers between devices, shards(): lax.all_to_all(shifted.astype(jnp.bfloat16).reshape(-1, width, tiles_here...  7.56 us
    all_to_all x1, starting transfers between devices, shards(): lax.all_to_all(jnp.stack([centre, tissue_sum, tissue_squares], axis=1).re...  6.7 us
  transfers between devices with their start and end apart: 3, of which 1 were waited for; matrix products, arithmetic and copies ran while one was open for 10% of the time, Pallas kernels for 0%

profile of v1, /device:TPU:44, one launch (start us, length us, event | category | flops | bytes accessed | tf_op | source)
XLA Modules:
  0.0 245.3 jit_solution(18027154383236739926)
XLA Ops:
  10.1 4.4 %multiply_reduce_fusion.2 = (f32[512]{0:T(512)S(1)}, f32[3136,512]{1,0:T(8,128)}) fusion(f32[3136]{0:T(1024)S(1)} %mul.122, bf16[3136,256]{1,0:T(8,128)(2,1)S(1)} %bitcast.20, bf16[256,512]{1,0:T(8,128)(2,1)} %param.10), kind=kOutput, calls=%fused_computation.9 | convolution fusion | flops 825294336 | bytes 8304896 | tf_op jit(solution)/shard_map/dot_general | solution.py:27
  14.5 9.7 %all-reduce.2 = (f32[512]{0:T(512)S(1)}, f32[]{:T(128)}) all-reduce(f32[512]{0:T(512)S(1)} %get-tuple-element.25, f32[]{:T(128)S(6)} %mul.125), channel_id=1, replica_groups=mesh['z'=4,'x'=4,'y'=4,'c'=2] {'z'}, use_global_device_ids=true, to_apply=%region_1.0 | all-reduce | flops 513 | bytes 4104 | tf_op jit(solution)/shard_map/psum | solution.py:14
  24.2 8.9 %all-reduce.1 = (f32[512]{0:T(512)S(1)}, f32[]{:T(128)}) all-reduce(f32[512]{0:T(512)S(1)} %get-tuple-element.11, f32[]{:T(128)} %get-tuple-element.12), channel_id=1, replica_groups=mesh['z'=4,'x'=4,'y'=4,'c'=2] {'x'}, use_global_device_ids=true, to_apply=%region_2.0 | all-reduce | flops 513 | bytes 4104 | tf_op jit(solution)/shard_map/psum | solution.py:14
  33.1 9.3 %all-reduce = (f32[512]{0:T(512)S(1)}, f32[]{:T(128)}) all-reduce(f32[512]{0:T(512)S(1)} %get-tuple-element.9, f32[]{:T(128)} %get-tuple-element.10), channel_id=1, replica_groups=mesh['z'=4,'x'=4,'y'=4,'c'=2] {'y'}, use_global_device_ids=true, to_apply=%region_3.0 | all-reduce | flops 513 | bytes 4104 | tf_op jit(solution)/shard_map/psum | solution.py:14
  42.4 3.1 %all-reduce.3 = (f32[512]{0:T(512)S(1)}, f32[]{:T(128)}) all-reduce(f32[512]{0:T(512)S(1)} %get-tuple-element.7, f32[]{:T(128)} %get-tuple-element.8), channel_id=1, replica_groups=mesh['z'=4,'x'=4,'y'=4,'c'=2] {'c'}, use_global_device_ids=true, to_apply=%region_4.0 | all-reduce | flops 513 | bytes 4104 | tf_op jit(solution)/shard_map/psum | solution.py:14
  46.1 3.6 %fusion.1 = f32[512]{0:T(512)S(1)} fusion(f32[3136,512]{1,0:T(8,128)} %get-tuple-element.26, f32[512]{0:T(512)S(1)} %broadcast_divide_fusion.1, f32[3136]{0:T(1024)S(1)} %mul.122), kind=kLoop, calls=%fused_computation.6 | loop fusion | flops 6422016 | bytes 6439168 | tf_op jit(solution)/shard_map/reduce_sum | solution.py:33
  49.7 10.6 %psum.106 = f32[512]{0:T(512)S(1)} all-reduce(f32[512]{0:T(512)S(1)} %fusion.1), channel_id=1, replica_groups=mesh['z'=4,'x'=4,'y'=4,'c'=2] {'z'}, use_global_device_ids=true, to_apply=%region_11.0 | all-reduce | flops 512 | bytes 4096 | tf_op jit(solution)/shard_map/psum | solution.py:14
  60.3 8.1 %psum.107 = f32[512]{0:T(512)S(1)} all-reduce(f32[512]{0:T(512)S(1)} %psum.106), channel_id=1, replica_groups=mesh['z'=4,'x'=4,'y'=4,'c'=2] {'x'}, use_global_device_ids=true, to_apply=%region_12.0 | all-reduce | flops 512 | bytes 4096 | tf_op jit(solution)/shard_map/psum | solution.py:14
  68.4 10.2 %psum.108 = f32[512]{0:T(512)S(1)} all-reduce(f32[512]{0:T(512)S(1)} %psum.107), channel_id=1, replica_groups=mesh['z'=4,'x'=4,'y'=4,'c'=2] {'y'}, use_global_device_ids=true, to_apply=%region_13.0 | all-reduce | flops 512 | bytes 4096 | tf_op jit(solution)/shard_map/psum | solution.py:14
  78.6 2.5 psum.109
  81.0 1.2 add_rsqrt_fusion
  82.2 11.4 %fusion.15 = (f32[1024]{0:T(1024)S(1)}, f32[3136,1024]{1,0:T(8,128)}) fusion(bf16[512,1024]{0,1:T(8,128)(2,1)} %all-gather.2.cloned.1.call-done, f32[3136,512]{1,0:T(8,128)} %get-tuple-element.26, f32[512]{0:T(512)S(1)} %copy-done.3, f32[512]{0:T(512)S(1)} %get-tuple-element.17, f32[512]{0:T(512)S(1)} %broadcast_divide_fusion.1, f32[512]{0:T(512)S(1)} %copy-done.4), kind=kOutput, calls=%fused_computation.36 | convolution fusion | flops 3301178368 | bytes 20328448 | tf_op jit(solution)/shard_map/dot_general | solution.py:38
  93.8 9.5 %multiply_reduce_fusion.1 = (f32[1024]{0:T(1024)S(1)}, f32[1024]{0:T(1024)S(1)}, bf16[1024,3136]{0,1:T(8,128)(2,1)}) fusion(f32[3136,1024]{1,0:T(8,128)} %get-tuple-element.28, f32[3136]{0:T(1024)S(1)} %mul.122, f32[1024]{0:T(1024)S(1)} %broadcast_multiply_fusion), kind=kLoop, calls=%fused_computation.2 | loop fusion | flops 22476800 | bytes 19292416 | tf_op jit(solution)/shard_map/reduce_sum | solution.py:43
  104.1 6.7 %all-to-all-start.1 = ((f32[32,32,3]{1,2,0:T(4,128)}), f32[32,32,3]{1,2,0:T(4,128)S(1)}, u32[]{:S(2)}, u32[]{:S(2)}) async-start(f32[32,32,3]{1,2,0:T(4,128)} %pad_maximum_fusion), calls=%async_computation.1 | async-start | bytes 131072 | tf_op jit(solution)/shard_map/all_to_all | solution.py:53
  110.8 9.2 %copy.17 = bf16[1024,3136]{1,0:T(8,128)(2,1)} copy(bf16[1024,3136]{0,1:T(8,128)(2,1)} %get-tuple-element.19) | data formatting | bytes 12845056 | tf_op jit(solution)/shard_map/convert_element_type | solution.py:47
  120.0 7.6 %all-to-all-start = ((bf16[32,32,3136]{2,1,0:T(8,128)(2,1)}), bf16[32,32,3136]{2,1,0:T(8,128)(2,1)}, u32[]{:S(2)}, u32[]{:S(2)}) async-start(bf16[32,32,3136]{2,1,0:T(8,128)(2,1)} %bitcast.21), calls=%async_computation | async-start | bytes 13107200 | tf_op jit(solution)/shard_map/all_to_all | solution.py:46
  127.8 0.8 dynamic_slice.14
  128.7 7.7 %psum.110 = f32[32]{0:T(128)S(1)} all-reduce(f32[32]{0:T(128)S(1)} %add_reduce_fusion), channel_id=1, replica_groups=mesh['z'=4,'x'=4,'y'=4,'c'=2] {'z'}, use_global_device_ids=true, to_apply=%region_20.0 | all-reduce | flops 32 | bytes 256 | tf_op jit(solution)/shard_map/psum | solution.py:14
  137.2 9.9 %psum.111 = f32[32]{0:T(128)S(1)} all-reduce(f32[32]{0:T(128)S(1)} %fusion.10), channel_id=1, replica_groups=mesh['z'=4,'x'=4,'y'=4,'c'=2] {'z'}, use_global_device_ids=true, to_apply=%region_22.0 | all-reduce | flops 32 | bytes 256 | tf_op jit(solution)/shard_map/psum | solution.py:14
  147.1 1.8 rsqrt_multiply_fusion
  149.0 67.8 %all-to-all-done = bf16[32,32,3136]{2,1,0:T(8,128)(2,1)} async-done(((bf16[32,32,3136]{2,1,0:T(8,128)(2,1)}), bf16[32,32,3136]{2,1,0:T(8,128)(2,1)}, u32[]{:S(2)}, u32[]{:S(2)}) %all-to-all-start) | async-done | bytes 6422560 | tf_op jit(solution)/shard_map/all_to_all | solution.py:46
  216.7 6.2 %fusion = bf16[32,32,3136]{2,0,1:T(8,128)(2,1)S(1)} fusion(bf16[32,32,3136]{2,1,0:T(8,128)(2,1)} %all-to-all-done, f32[32]{0:T(128)S(1)} %dynamic_slice.14, f32[32]{0:T(128)S(1)} %get-tuple-element.15, f32[32,32]{1,0:T(8,128)S(1)} %subtract_bitcast_fusion), kind=kLoop, calls=%fused_computation.5 | loop fusion | flops 19267584 | bytes 12849408 | tf_op jit(solution)/shard_map/transpose | solution.py:76
  223.0 4.7 %copy.20 = bf16[32,32,3136]{2,1,0:T(8,128)(2,1)} copy(bf16[32,32,3136]{2,0,1:T(8,128)(2,1)S(1)} %fusion) | data formatting | bytes 12845056 | tf_op jit(solution)/shard_map/transpose | solution.py:76
  227.7 10.8 %reshape.64 = bf16[1,32,100352]{2,1,0:T(8,128)(2,1)} reshape(bf16[32,32,3136]{2,1,0:T(8,128)(2,1)} %copy.20) | data formatting | bytes 12845056 | tf_op jit(solution)/shard_map/reshape | solution.py:76
  (35 shorter events, 4.9 us)
Async XLA Ops:
  7.2 2.9 %copy-start = (bf16[1,4,784,256]{3,2,1,0:T(8,128)(2,1)S(1)}, bf16[1,4,784,256]{3,2,1,0:T(8,128)(2,1)}, u32[]{:S(2)}) copy-start(bf16[1,4,784,256]{3,2,1,0:T(8,128)(2,1)} %param.8) | copy-start | bytes 4816900
  7.2 75.1 %all-gather.2.cloned.1.call-start = ((), (), s32[]{:S(2)}) async-start(), calls=%async_computation.2 | async-start | bytes 1081344 | tf_op jit(solution)/shard_map/all_gather | solution.py:37
  14.5 67.7 %copy-start.3 = (f32[512]{0:T(512)S(1)}, f32[512]{0:T(512)}, u32[]{:S(2)}) copy-start(f32[512]{0:T(512)} %param.12) | copy-start | bytes 6148
  14.5 67.7 %copy-start.4 = (f32[512]{0:T(512)S(1)}, f32[512]{0:T(512)}, u32[]{:S(2)}) copy-start(f32[512]{0:T(512)} %param.11) | copy-start | bytes 6148
  46.1 47.6 %copy-start.1 = (f32[512]{0:T(512)}, f32[512]{0:T(512)S(1)}, u32[]{:S(2)}) copy-start(f32[512]{0:T(512)S(1)} %broadcast_divide_fusion.1) | copy-start | bytes 6148
  104.1 15.9 %all-to-all-start.1 = ((f32[32,32,3]{1,2,0:T(4,128)}), f32[32,32,3]{1,2,0:T(4,128)S(1)}, u32[]{:S(2)}, u32[]{:S(2)}) async-start(f32[32,32,3]{1,2,0:T(4,128)} %pad_maximum_fusion), calls=%async_computation.1 | async-start | bytes 131072 | tf_op jit(solution)/shard_map/all_to_all | solution.py:53
  120.0 7.6 %copy-start.5 = (s32[1,128]{1,0:T(1,128)S(1)}, s32[1,128]{1,0:T(1,128)}, u32[]{:S(2)}) copy-start(s32[1,128]{1,0:T(1,128)} %param.9) | copy-start | bytes 1540
  120.0 96.7 %all-to-all-start = ((bf16[32,32,3136]{2,1,0:T(8,128)(2,1)}), bf16[32,32,3136]{2,1,0:T(8,128)(2,1)}, u32[]{:S(2)}, u32[]{:S(2)}) async-start(bf16[32,32,3136]{2,1,0:T(8,128)(2,1)} %bitcast.21), calls=%async_computation | async-start | bytes 13107200 | tf_op jit(solution)/shard_map/all_to_all | solution.py:46
  137.1 85.9 %copy-start.2 = (f32[32]{0:T(128)}, f32[32]{0:T(128)S(1)}, u32[]{:S(2)}) copy-start(f32[32]{0:T(128)S(1)} %broadcast_divide_fusion.3) | copy-start | bytes 388
Sparse Core Ops, SparseCore 0:
  10.2 42.4 all-gather.1
